TPU v7x, 256 devices: a whole 4x4x8 slice. The times are simulated.
256 devices in a mesh: gx: 8 (over x, core), gy: 32 (over y, z).
Axes of the slice: x: 4, y: 4, z: 8, core: 2. Of those that a mesh axis runs over, the one named last changes fastest.
Arguments:
- fields: bfloat16 [672, 672, 1536], P('gx', 'gy'), may hold values from -16 to 16
- x_factor: bfloat16 [672, 336], replicated, may hold values from -0.00030517578 to 0.00030517578
- running_r: float32 [672, 672], replicated, as said below
Outputs:
- new_r: float32 [672, 672], P('gy', 'gx')
Inputs may be any that keep to these rules, and one draw needn't show every extreme that they name: `running_r`: upper triangular with a positive diagonal.
All inputs are finite; a program needn't handle non-finite values.
Results may differ from a plain program's by a relative error of at most 0.0003.
Values may be sent and summed in bfloat16 or wider, within the bound.
A program may use at most 256 MiB of HBM per device.

v0:
```python
import jax
import jax.numpy as jnp
from jax import lax
from jax.sharding import PartitionSpec as P


def fibre_gram(fibres):
    local_gram = lax.dot_general(
        fibres, fibres, (((0, 2), (0, 2)), ((), ())), preferred_element_type=jnp.float32
    )
    return lax.psum(local_gram, ("gx", "gy"))


def project_local(x_factor, block):
    full_x = block.shape[0]
    middle = block.shape[1]
    part_cells = block.shape[2]
    product = lax.dot_general(
        x_factor,
        block.reshape(full_x, middle * part_cells),
        (((0,), (0,)), ((), ())),
        preferred_element_type=jnp.float32,
    )
    return product.astype(jnp.bfloat16).reshape(x_factor.shape[1], middle, part_cells)


def on_device(fields, x_factor, running_r):
    full_y = running_r.shape[0]
    exchanged = lax.all_to_all(fields, "gx", split_axis=2, concat_axis=0, tiled=True)
    projected = project_local(x_factor, exchanged)
    fibres = lax.all_to_all(projected, "gy", split_axis=2, concat_axis=1, tiled=True)
    gram_sum = fibre_gram(fibres)
    total = (
        jnp.dot(
            running_r.T,
            running_r,
            precision=lax.Precision.HIGHEST,
            preferred_element_type=jnp.float32,
        )
        + gram_sum
    )
    upper_r = jnp.linalg.cholesky(total).T
    row_block = full_y // lax.axis_size("gy")
    col_block = full_y // lax.axis_size("gx")
    return lax.dynamic_slice(
        upper_r,
        (lax.axis_index("gy") * row_block, lax.axis_index("gx") * col_block),
        (row_block, col_block),
    )


def solution(mesh):
    in_specs = (P("gx", "gy", None), P(), P())
    out_specs = P("gy", "gx")
    return jax.shard_map(
        on_device, mesh=mesh, in_specs=in_specs, out_specs=out_specs, check_vma=False
    )
```

profile of v0, /device:TPU:2, one launch (start us, length us, event | category | flops | bytes accessed | tf_op | source)
XLA Modules:
  0.0 698.8 jit_solution(13633956588699801760)
XLA Ops:
  6.5 11.8 %copy.19 = bf16[84,21,1536]{0,1,2:T(8,128)(2,1)} copy(bf16[84,21,1536]{2,0,1:T(8,128)(2,1)} %param.3) | data formatting | bytes 10838016 | tf_op args[0]
  18.4 114.1 %all_to_all.33 = bf16[84,21,1536]{0,1,2:T(8,128)(2,1)} all-to-all(bf16[84,21,1536]{0,1,2:T(8,128)(2,1)} %copy.19), channel_id=1, replica_groups=mesh['gx'=8,'gy'=32] {'gx'}, dimensions={2} | all-to-all | bytes 10838016 | tf_op jit(solution)/shard_map/all_to_all | solution.py:29
  132.5 15.4 %copy.20 = bf16[84,21,8,192]{3,1,0,2:T(8,128)(2,1)} copy(bf16[84,21,8,192]{0,1,3,2:T(8,128)(2,1)} %bitcast.50) | data formatting | bytes 10838016 | tf_op jit(solution)/shard_map/all_to_all | solution.py:29
  147.9 12.5 %reshape.46 = bf16[672,4032]{1,0:T(8,128)(2,1)} reshape(bf16[8,84,21,192]{3,2,1,0:T(8,128)(2,1)} %bitcast.51) | data formatting | bytes 10838016 | tf_op jit(solution)/shard_map/reshape | solution.py:20
  160.4 6.4 convolution_convert_fusion
  166.8 4.5 copy.21
  171.3 3.7 copy.22
  175.1 91.4 %all_to_all.34 = bf16[336,21,192]{0,1,2:T(8,128)(2,1)S(1)} all-to-all(bf16[336,21,192]{0,1,2:T(8,128)(2,1)S(1)} %copy.22), channel_id=1, replica_groups=mesh['gx'=8,'gy'=32] {'gy'}, dimensions={2} | all-to-all | bytes 5419008 | tf_op jit(solution)/shard_map/all_to_all | solution.py:31
  266.5 2.2 copy.23
  268.7 6.0 all_to_all.30
  274.7 6.8 convolution_bitcast_fusion
  281.5 257.3 %all-reduce.3.cloned.1.call-done = f32[672,672]{0,1:T(8,128)} async-done(((f32[672,672]{0,1:T(8,128)}), f32[672,672]{0,1:T(8,128)}) %all-reduce.3.cloned.1.call-update) | async-done | bytes 1806352 | tf_op jit(solution)/shard_map/psum | solution.py:11
  538.8 8.2 %convolution_add_fusion = f32[672,672]{0,1:T(8,128)} fusion(f32[672,672]{0,1:T(8,128)} %all-reduce.3.cloned.1.call-done, f32[672,672]{1,0:T(8,128)S(1)} %copy-done), kind=kOutput, calls=%fused_computation.4 | convolution fusion | flops 3642024960 | bytes 5419008 | tf_op jit(solution)/shard_map/dot_general | solution.py:34
  547.0 3.1 copy.27
  550.2 2.5 fusion
  552.7 1.3 copy-done.1
  554.0 11.7 %cholesky.166 = f32[128,128]{1,0:T(8,128)S(1)} custom-call(f32[128,128]{1,0:T(8,128)S(1)} %cholesky.430), custom_call_target="Cholesky" | custom-call | tf_op jit(solution)/shard_map/jit(cholesky)/cholesky | solution.py:42
  565.7 9.8 %custom-call.43 = f32[1,128,128]{1,2,0:T(8,128)S(1)} custom-call(f32[1,128,128]{2,1,0:T(8,128)S(1)} %get-tuple-element.18), custom_call_target="InvertDiagBlocksLowerTriangular" | custom-call | tf_op jit(solution)/shard_map/jit(cholesky)/cholesky | solution.py:42
  575.6 1.4 cholesky.342
  577.0 2.1 constant_dynamic-update-slice_fusion.4
  579.0 1.3 convolution_subtract_fusion
  580.4 11.7 %cholesky.189 = f32[128,128]{1,0:T(8,128)S(1)} custom-call(f32[128,128]{1,0:T(8,128)S(1)} %cholesky.434), custom_call_target="Cholesky" | custom-call | tf_op jit(solution)/shard_map/jit(cholesky)/cholesky | solution.py:42
  592.1 0.7 select_reduce_fusion.3
  592.8 10.2 %custom-call.44 = f32[1,128,128]{1,2,0:T(8,128)S(1)} custom-call(f32[1,128,128]{2,1,0:T(8,128)S(1)} %get-tuple-element.15), custom_call_target="InvertDiagBlocksLowerTriangular" | custom-call | tf_op jit(solution)/shard_map/jit(cholesky)/cholesky | solution.py:42
  603.0 1.0 convolution_dynamic-update-slice_fusion
  604.0 1.6 convolution_subtract_fusion.1
  605.6 11.7 %cholesky.356 = f32[128,128]{1,0:T(8,128)S(1)} custom-call(f32[128,128]{1,0:T(8,128)S(1)} %cholesky.439), custom_call_target="Cholesky" | custom-call | tf_op jit(solution)/shard_map/jit(cholesky)/cholesky | solution.py:42
  618.0 0.7 compare_reduce_fusion.3
  618.7 9.8 %custom-call.45 = f32[1,128,128]{1,2,0:T(8,128)S(1)} custom-call(f32[1,128,128]{2,1,0:T(8,128)S(1)} %get-tuple-element.12), custom_call_target="InvertDiagBlocksLowerTriangular" | custom-call | tf_op jit(solution)/shard_map/jit(cholesky)/cholesky | solution.py:42
  628.5 1.0 convolution_dynamic-update-slice_fusion.1
  629.4 1.7 convolution_subtract_fusion.2
  631.1 11.8 %cholesky.375 = f32[128,128]{1,0:T(8,128)S(1)} custom-call(f32[128,128]{1,0:T(8,128)S(1)} %cholesky.444), custom_call_target="Cholesky" | custom-call | tf_op jit(solution)/shard_map/jit(cholesky)/cholesky | solution.py:42
  643.0 0.6 select_reduce_fusion.1
  643.6 0.7 compare_reduce_fusion.2
  644.3 9.8 %custom-call.46 = f32[1,128,128]{1,2,0:T(8,128)S(1)} custom-call(f32[1,128,128]{2,1,0:T(8,128)S(1)} %get-tuple-element.9), custom_call_target="InvertDiagBlocksLowerTriangular" | custom-call | tf_op jit(solution)/shard_map/jit(cholesky)/cholesky | solution.py:42
  654.1 0.9 convolution_dynamic-update-slice_fusion.2
  655.0 1.5 convolution_subtract_fusion.3
  656.5 11.7 %cholesky.394 = f32[128,128]{1,0:T(8,128)S(1)} custom-call(f32[128,128]{1,0:T(8,128)S(1)} %cholesky.449), custom_call_target="Cholesky" | custom-call | tf_op jit(solution)/shard_map/jit(cholesky)/cholesky | solution.py:42
  668.2 0.6 select_reduce_fusion
  668.9 0.7 compare_reduce_fusion.1
  669.5 9.8 %custom-call.47 = f32[1,128,128]{1,2,0:T(8,128)S(1)} custom-call(f32[1,128,128]{2,1,0:T(8,128)S(1)} %get-tuple-element.6), custom_call_target="InvertDiagBlocksLowerTriangular" | custom-call | tf_op jit(solution)/shard_map/jit(cholesky)/cholesky | solution.py:42
  679.3 0.8 convolution_dynamic-update-slice_fusion.3
  680.1 1.2 convolution_subtract_fusion.4
  681.3 2.9 cholesky.415
  684.8 0.7 compare_reduce_fusion
  685.6 0.6 compare_reduce_fusion.4
  690.0 1.0 fusion.20
  691.0 0.7 copy.28
  (15 shorter events, 1.3 us)
Async XLA Ops:
  6.5 532.3 %copy-start = (f32[672,672]{1,0:T(8,128)S(1)}, f32[672,672]{1,0:T(8,128)}, u32[]{:S(2)}) copy-start(f32[672,672]{1,0:T(8,128)} %param.5) | copy-start | bytes 5419012
  6.5 532.3 %all-reduce.3.cloned.1.call-start = ((), (), s32[]{:S(2)}) async-start(), calls=%async_computation.2 | async-start | bytes 4128768 | tf_op jit(solution)/shard_map/psum | solution.py:11
  147.9 12.5 %copy-start.2 = (bf16[672,336]{1,0:T(8,128)(2,1)S(1)}, bf16[672,336]{1,0:T(8,128)(2,1)}, u32[]{:S(2)}) copy-start(bf16[672,336]{1,0:T(8,128)(2,1)} %param.4) | copy-start | bytes 1354756
  552.6 1.3 copy-start.1
Sparse Core Ops, SparseCore 0:
  281.6 257.1 all-reduce.2
where the time goes:
time: 706 us; the launch traced here: 699 us
  waiting for transfers between devices  257 us (36%)
  blocking collectives  206 us (29%)
  other arithmetic  121 us (17%)
  local copies, waits for them, and re-layouts  62.8 us (9%)
  matrix products  34.5 us (5%)
  between operations  17.6 us (2%)
    psum x1, waiting for transfers between devices, fibre_gram(): return lax.psum(local_gram, ('gx', 'gy'))  257 us
    another operation x22, other arithmetic, on_device(): upper_r = jnp.linalg.cholesky(total).T  118 us
    all_to_all x1, blocking collectives, on_device(): lax.all_to_all(fields, 'gx', split_axis=2, concat_axis=0, tiled=True)  114 us
    all_to_all x1, blocking collectives, on_device(): lax.all_to_all(projected, 'gy', split_axis=2, concat_axis=1, tiled=True)  91.4 us
    all_to_all x1, local copies, waits for them, and re-layouts, on_device(): lax.all_to_all(fields, 'gx', split_axis=2, concat_axis=0, tiled=True)  15.4 us
  transfers between devices with their start and end apart: 1, of which 1 were waited for; matrix products, arithmetic and copies ran while one was open for 0% of the time, Pallas kernels for 0%

commit v1 on v0

--- a/solution.py
+++ b/solution.py
@@ -8,7 +8,7 @@
     local_gram = lax.dot_general(
         fibres, fibres, (((0, 2), (0, 2)), ((), ())), preferred_element_type=jnp.float32
     )
-    return lax.psum(local_gram, ("gx", "gy"))
+    return lax.psum(lax.psum(local_gram, "gx"), "gy")
 
 
 def project_local(x_factor, block):

time: 706 us -> 672 us (0.952)
  waiting for transfers between devices: 257 us -> 222 us
    psum x1 -> x2, waiting for transfers between devices: 257 us -> 222 us  [fibre_gram(): return lax.psum(lax.psum(local_gram, 'gx'), 'gy')]
  transfers between devices with their start and end apart: 1 -> 2, of which waited for: 1 -> 2; matrix products, arithmetic and copies ran while one was open for 0% -> 0% of each run, Pallas kernels for 0% -> 0%
where the time goes in v1:
time: 672 us; the launch traced here: 664 us
  waiting for transfers between devices  222 us (33%)
  blocking collectives  205 us (31%)
  other arithmetic  121 us (18%)
  local copies, waits for them, and re-layouts  62.7 us (9%)
  matrix products  34.5 us (5%)
  between operations  17.6 us (3%)
    psum x2, waiting for transfers between devices, fibre_gram(): return lax.psum(lax.psum(local_gram, 'gx'), 'gy')  222 us
    another operation x22, other arithmetic, on_device(): upper_r = jnp.linalg.cholesky(total).T  118 us
    all_to_all x1, blocking collectives, on_device(): lax.all_to_all(fields, 'gx', split_axis=2, concat_axis=0, tiled=True)  114 us
    all_to_all x1, blocking collectives, on_device(): lax.all_to_all(projected, 'gy', split_axis=2, concat_axis=1, tiled=True)  91.2 us
    all_to_all x1, local copies, waits for them, and re-layouts, on_device(): lax.all_to_all(fields, 'gx', split_axis=2, concat_axis=0, tiled=True)  15.4 us
  transfers between devices with their start and end apart: 2, of which 2 were waited for; matrix products, arithmetic and copies ran while one was open for 0% of the time, Pallas kernels for 0%

profile of v1, /device:TPU:2, one launch (start us, length us, event | category | flops | bytes accessed | tf_op | source)
XLA Modules:
  0.0 664.0 jit_solution(2034544013017403192)
XLA Ops:
  6.5 11.8 %copy.19 = bf16[84,21,1536]{0,1,2:T(8,128)(2,1)} copy(bf16[84,21,1536]{2,0,1:T(8,128)(2,1)} %param.3) | data formatting | bytes 10838016 | tf_op args[0]
  18.4 114.1 %all_to_all.33 = bf16[84,21,1536]{0,1,2:T(8,128)(2,1)} all-to-all(bf16[84,21,1536]{0,1,2:T(8,128)(2,1)} %copy.19), channel_id=1, replica_groups=mesh['gx'=8,'gy'=32] {'gx'}, dimensions={2} | all-to-all | bytes 10838016 | tf_op jit(solution)/shard_map/all_to_all | solution.py:29
  132.5 15.4 %copy.20 = bf16[84,21,8,192]{3,1,0,2:T(8,128)(2,1)} copy(bf16[84,21,8,192]{0,1,3,2:T(8,128)(2,1)} %bitcast.50) | data formatting | bytes 10838016 | tf_op jit(solution)/shard_map/all_to_all | solution.py:29
  147.9 12.5 %reshape.46 = bf16[672,4032]{1,0:T(8,128)(2,1)} reshape(bf16[8,84,21,192]{3,2,1,0:T(8,128)(2,1)} %bitcast.51) | data formatting | bytes 10838016 | tf_op jit(solution)/shard_map/reshape | solution.py:20
  160.4 6.4 convolution_convert_fusion
  166.8 4.5 copy.21
  171.3 3.7 copy.22
  175.1 91.2 %all_to_all.34 = bf16[336,21,192]{0,1,2:T(8,128)(2,1)S(1)} all-to-all(bf16[336,21,192]{0,1,2:T(8,128)(2,1)S(1)} %copy.22), channel_id=1, replica_groups=mesh['gx'=8,'gy'=32] {'gy'}, dimensions={2} | all-to-all | bytes 5419008 | tf_op jit(solution)/shard_map/all_to_all | solution.py:31
  266.3 2.2 copy.23
  268.5 6.0 all_to_all.30
  274.5 6.8 %convolution_bitcast_fusion = f32[672,672]{0,1:T(8,128)} fusion(bf16[336,672,6]{0,1,2:T(8,128)(2,1)} %all_to_all.30), kind=kOutput, calls=%fused_computation.3 | convolution fusion | flops 1820786688 | bytes 4515840 | tf_op jit(solution)/shard_map/dot_general | solution.py:8
  281.6 63.8 %all-reduce.4.cloned.1.call-done = f32[672,672]{0,1:T(8,128)} async-done(((f32[672,672]{0,1:T(8,128)}), f32[672,672]{0,1:T(8,128)}) %all-reduce.4.cloned.1.call-update) | async-done | bytes 1806352 | tf_op jit(solution)/shard_map/psum | solution.py:11
  345.4 158.6 %all-reduce.6.cloned.1.call-done = f32[672,672]{0,1:T(8,128)} async-done(((f32[672,672]{0,1:T(8,128)}), f32[672,672]{0,1:T(8,128)}) %all-reduce.6.cloned.1.call-update) | async-done | bytes 1806352 | tf_op jit(solution)/shard_map/psum | solution.py:11
  504.0 8.3 %convolution_add_fusion = f32[672,672]{0,1:T(8,128)} fusion(f32[672,672]{0,1:T(8,128)} %all-reduce.6.cloned.1.call-done, f32[672,672]{1,0:T(8,128)S(1)} %copy-done), kind=kOutput, calls=%fused_computation.4 | convolution fusion | flops 3642024960 | bytes 5419008 | tf_op jit(solution)/shard_map/dot_general | solution.py:34
  512.3 3.1 copy.27
  515.4 2.5 fusion
  517.9 1.3 copy-done.1
  519.2 11.7 %cholesky.166 = f32[128,128]{1,0:T(8,128)S(1)} custom-call(f32[128,128]{1,0:T(8,128)S(1)} %cholesky.430), custom_call_target="Cholesky" | custom-call | tf_op jit(solution)/shard_map/jit(cholesky)/cholesky | solution.py:42
  531.0 9.8 %custom-call.43 = f32[1,128,128]{1,2,0:T(8,128)S(1)} custom-call(f32[1,128,128]{2,1,0:T(8,128)S(1)} %get-tuple-element.18), custom_call_target="InvertDiagBlocksLowerTriangular" | custom-call | tf_op jit(solution)/shard_map/jit(cholesky)/cholesky | solution.py:42
  540.8 1.4 cholesky.342
  542.2 2.1 constant_dynamic-update-slice_fusion.4
  544.3 1.3 convolution_subtract_fusion
  545.6 11.7 %cholesky.189 = f32[128,128]{1,0:T(8,128)S(1)} custom-call(f32[128,128]{1,0:T(8,128)S(1)} %cholesky.434), custom_call_target="Cholesky" | custom-call | tf_op jit(solution)/shard_map/jit(cholesky)/cholesky | solution.py:42
  557.4 0.7 select_reduce_fusion.3
  558.0 10.2 %custom-call.44 = f32[1,128,128]{1,2,0:T(8,128)S(1)} custom-call(f32[1,128,128]{2,1,0:T(8,128)S(1)} %get-tuple-element.15), custom_call_target="InvertDiagBlocksLowerTriangular" | custom-call | tf_op jit(solution)/shard_map/jit(cholesky)/cholesky | solution.py:42
  568.2 1.0 convolution_dynamic-update-slice_fusion
  569.2 1.6 convolution_subtract_fusion.1
  570.9 11.7 %cholesky.356 = f32[128,128]{1,0:T(8,128)S(1)} custom-call(f32[128,128]{1,0:T(8,128)S(1)} %cholesky.439), custom_call_target="Cholesky" | custom-call | tf_op jit(solution)/shard_map/jit(cholesky)/cholesky | solution.py:42
  583.2 0.7 compare_reduce_fusion.3
  583.9 9.8 %custom-call.45 = f32[1,128,128]{1,2,0:T(8,128)S(1)} custom-call(f32[1,128,128]{2,1,0:T(8,128)S(1)} %get-tuple-element.12), custom_call_target="InvertDiagBlocksLowerTriangular" | custom-call | tf_op jit(solution)/shard_map/jit(cholesky)/cholesky | solution.py:42
  593.7 0.9 convolution_dynamic-update-slice_fusion.1
  594.7 1.7 convolution_subtract_fusion.2
  596.3 11.8 %cholesky.375 = f32[128,128]{1,0:T(8,128)S(1)} custom-call(f32[128,128]{1,0:T(8,128)S(1)} %cholesky.444), custom_call_target="Cholesky" | custom-call | tf_op jit(solution)/shard_map/jit(cholesky)/cholesky | solution.py:42
  608.2 0.6 select_reduce_fusion.1
  608.8 0.7 compare_reduce_fusion.2
  609.6 9.8 %custom-call.46 = f32[1,128,128]{1,2,0:T(8,128)S(1)} custom-call(f32[1,128,128]{2,1,0:T(8,128)S(1)} %get-tuple-element.9), custom_call_target="InvertDiagBlocksLowerTriangular" | custom-call | tf_op jit(solution)/shard_map/jit(cholesky)/cholesky | solution.py:42
  619.4 0.9 convolution_dynamic-update-slice_fusion.2
  620.2 1.5 convolution_subtract_fusion.3
  621.7 11.7 %cholesky.394 = f32[128,128]{1,0:T(8,128)S(1)} custom-call(f32[128,128]{1,0:T(8,128)S(1)} %cholesky.449), custom_call_target="Cholesky" | custom-call | tf_op jit(solution)/shard_map/jit(cholesky)/cholesky | solution.py:42
  633.5 0.6 select_reduce_fusion
  634.1 0.7 compare_reduce_fusion.1
  634.8 9.8 %custom-call.47 = f32[1,128,128]{1,2,0:T(8,128)S(1)} custom-call(f32[1,128,128]{2,1,0:T(8,128)S(1)} %get-tuple-element.6), custom_call_target="InvertDiagBlocksLowerTriangular" | custom-call | tf_op jit(solution)/shard_map/jit(cholesky)/cholesky | solution.py:42
  644.6 0.8 convolution_dynamic-update-slice_fusion.3
  645.4 1.2 convolution_subtract_fusion.4
  646.5 2.9 cholesky.415
  650.1 0.7 compare_reduce_fusion
  655.3 1.0 fusion.20
  656.3 0.7 copy.28
  (18 shorter events, 2.2 us)
Async XLA Ops:
  6.5 497.5 %copy-start = (f32[672,672]{1,0:T(8,128)S(1)}, f32[672,672]{1,0:T(8,128)}, u32[]{:S(2)}) copy-start(f32[672,672]{1,0:T(8,128)} %param.5) | copy-start | bytes 5419012
  6.5 338.9 %all-reduce.4.cloned.1.call-start = ((), (), s32[]{:S(2)}) async-start(), calls=%async_computation.2 | async-start | bytes 4128768 | tf_op jit(solution)/shard_map/psum | solution.py:11
  147.9 12.5 %copy-start.2 = (bf16[672,336]{1,0:T(8,128)(2,1)S(1)}, bf16[672,336]{1,0:T(8,128)(2,1)}, u32[]{:S(2)}) copy-start(bf16[672,336]{1,0:T(8,128)(2,1)} %param.4) | copy-start | bytes 1354756
  281.3 222.7 %all-reduce.6.cloned.1.call-start = ((), (), s32[]{:S(2)}) async-start(), calls=%async_computation.3 | async-start | bytes 4128768 | tf_op jit(solution)/shard_map/psum | solution.py:11
  517.9 1.3 copy-start.1
Sparse Core Ops, SparseCore 0:
  281.5 63.9 all-reduce.3
  348.9 155.1 all-reduce.5

commit v2 on v0

--- a/solution.py
+++ b/solution.py
@@ -26,7 +26,10 @@
 
 def on_device(fields, x_factor, running_r):
     full_y = running_r.shape[0]
-    exchanged = lax.all_to_all(fields, "gx", split_axis=2, concat_axis=0, tiled=True)
+    exchanged = jnp.concatenate(
+        lax.all_to_all(jnp.stack(jnp.split(fields, lax.axis_size("gx"), axis=2)), "gx", 0, 0),
+        axis=0,
+    )
     projected = project_local(x_factor, exchanged)
     fibres = lax.all_to_all(projected, "gy", split_axis=2, concat_axis=1, tiled=True)
     gram_sum = fibre_gram(fibres)

time: 706 us -> 672 us (0.952)
  blocking collectives: 206 us -> 183 us
  local copies, waits for them, and re-layouts: 62.8 us -> 49.8 us
    all_to_all x1, blocking collectives: 114 us -> 91.3 us  [on_device(): lax.all_to_all(jnp.stack(jnp.split(fields, lax.axis_size('gx'), axis=2)),...]
    another operation x0 -> x2, local copies, waits for them, and re-layouts: none -> 12.9 us  [the longest x1 12.5 us: project_local(): block.reshape(full_x, middle * part_cells)]
    reshape x1 -> x0, local copies, waits for them, and re-layouts: 12.5 us -> none  [project_local(): block.reshape(full_x, middle * part_cells)]
    all_to_all x1, local copies, waits for them, and re-layouts: 15.4 us -> 8.03 us  [on_device(): lax.all_to_all(jnp.stack(jnp.split(fields, lax.axis_size('gx'), axis=2)),...]
where the time goes in v2:
time: 672 us; the launch traced here: 664 us
  waiting for transfers between devices  257 us (38%)
  blocking collectives  183 us (27%)
  other arithmetic  121 us (18%)
  local copies, waits for them, and re-layouts  49.8 us (7%)
  matrix products  34.6 us (5%)
  between operations  17.6 us (3%)
    psum x1, waiting for transfers between devices, fibre_gram(): return lax.psum(local_gram, ('gx', 'gy'))  257 us
    another operation x22, other arithmetic, on_device(): upper_r = jnp.linalg.cholesky(total).T  118 us
    all_to_all x1, blocking collectives, on_device(): lax.all_to_all(projected, 'gy', split_axis=2, concat_axis=1, tiled=True)  92.1 us
    all_to_all x1, blocking collectives, on_device(): lax.all_to_all(jnp.stack(jnp.split(fields, lax.axis_size('gx'), axis=2)),...  91.3 us
  transfers between devices with their start and end apart: 1, of which 1 were waited for; matrix products, arithmetic and copies ran while one was open for 0% of the time, Pallas kernels for 0%

profile of v2, /device:TPU:2, one launch (start us, length us, event | category | flops | bytes accessed | tf_op | source)
XLA Modules:
  0.0 663.8 jit_solution(7904213924808287970)
XLA Ops:
  6.5 1.4 bitcast_dynamic-update-slice_fusion.7
  7.9 2.2 bitcast_dynamic-update-slice_fusion.6
  10.1 1.3 bitcast_dynamic-update-slice_fusion.5
  12.7 91.3 %all_to_all.23 = bf16[8,84,21,192]{3,1,2,0:T(8,128)(2,1)} all-to-all(bf16[8,84,21,192]{3,1,2,0:T(8,128)(2,1)S(1)} %bitcast_dynamic-update-slice_fusion), channel_id=1, replica_groups=mesh['gx'=8,'gy'=32] {'gx'}, dimensions={0} | all-to-all | bytes 10838016 | tf_op jit(solution)/shard_map/all_to_all | solution.py:30
  104.0 8.0 %copy.19 = bf16[8,84,21,192]{3,2,1,0:T(8,128)(2,1)} copy(bf16[8,84,21,192]{3,1,2,0:T(8,128)(2,1)} %all_to_all.23) | data formatting | bytes 10838016 | tf_op jit(solution)/shard_map/all_to_all | solution.py:30
  112.1 12.5 %reshape_reshape.3 = bf16[672,4032]{1,0:T(8,128)(2,1)} reshape(bf16[8,84,21,192]{3,2,1,0:T(8,128)(2,1)} %copy.19) | data formatting | bytes 10838016 | tf_op jit(solution)/shard_map/reshape;reshape | solution.py:20
  124.6 6.5 fusion
  131.1 4.5 copy.20
  135.6 3.7 copy.21
  139.4 92.1 %all_to_all.24 = bf16[336,21,192]{0,1,2:T(8,128)(2,1)S(1)} all-to-all(bf16[336,21,192]{0,1,2:T(8,128)(2,1)S(1)} %copy.21), channel_id=1, replica_groups=mesh['gx'=8,'gy'=32] {'gy'}, dimensions={2} | all-to-all | bytes 5419008 | tf_op jit(solution)/shard_map/all_to_all | solution.py:34
  231.5 2.2 copy.22
  233.7 6.0 all_to_all.20
  239.7 6.8 %convolution_bitcast_fusion = f32[672,672]{0,1:T(8,128)} fusion(bf16[336,672,6]{0,1,2:T(8,128)(2,1)} %all_to_all.20), kind=kOutput, calls=%fused_computation.4 | convolution fusion | flops 1820786688 | bytes 4515840 | tf_op jit(solution)/shard_map/dot_general | solution.py:8
  246.5 257.3 %all-reduce.3.cloned.1.call-done = f32[672,672]{0,1:T(8,128)} async-done(((f32[672,672]{0,1:T(8,128)}), f32[672,672]{0,1:T(8,128)}) %all-reduce.3.cloned.1.call-update) | async-done | bytes 1806352 | tf_op jit(solution)/shard_map/psum | solution.py:11
  503.9 8.2 %convolution_add_fusion = f32[672,672]{0,1:T(8,128)} fusion(f32[672,672]{0,1:T(8,128)} %all-reduce.3.cloned.1.call-done, f32[672,672]{1,0:T(8,128)S(1)} %copy-done), kind=kOutput, calls=%fused_computation.5 | convolution fusion | flops 3642024960 | bytes 5419008 | tf_op jit(solution)/shard_map/dot_general | solution.py:37
  512.1 3.1 copy.26
  515.3 2.5 fusion.1
  517.7 1.3 copy-done.2
  519.1 11.7 %cholesky.166 = f32[128,128]{1,0:T(8,128)S(1)} custom-call(f32[128,128]{1,0:T(8,128)S(1)} %cholesky.430), custom_call_target="Cholesky" | custom-call | tf_op jit(solution)/shard_map/jit(cholesky)/cholesky | solution.py:45
  530.8 9.8 %custom-call.43 = f32[1,128,128]{1,2,0:T(8,128)S(1)} custom-call(f32[1,128,128]{2,1,0:T(8,128)S(1)} %get-tuple-element.18), custom_call_target="InvertDiagBlocksLowerTriangular" | custom-call | tf_op jit(solution)/shard_map/jit(cholesky)/cholesky | solution.py:45
  540.6 1.4 cholesky.342
  542.1 2.1 constant_dynamic-update-slice_fusion.4
  544.1 1.3 convolution_subtract_fusion
  545.5 11.7 %cholesky.189 = f32[128,128]{1,0:T(8,128)S(1)} custom-call(f32[128,128]{1,0:T(8,128)S(1)} %cholesky.434), custom_call_target="Cholesky" | custom-call | tf_op jit(solution)/shard_map/jit(cholesky)/cholesky | solution.py:45
  557.2 0.7 select_reduce_fusion.3
  557.9 10.2 %custom-call.44 = f32[1,128,128]{1,2,0:T(8,128)S(1)} custom-call(f32[1,128,128]{2,1,0:T(8,128)S(1)} %get-tuple-element.15), custom_call_target="InvertDiagBlocksLowerTriangular" | custom-call | tf_op jit(solution)/shard_map/jit(cholesky)/cholesky | solution.py:45
  568.0 1.0 convolution_dynamic-update-slice_fusion
  569.1 1.6 convolution_subtract_fusion.1
  570.7 11.7 %cholesky.356 = f32[128,128]{1,0:T(8,128)S(1)} custom-call(f32[128,128]{1,0:T(8,128)S(1)} %cholesky.439), custom_call_target="Cholesky" | custom-call | tf_op jit(solution)/shard_map/jit(cholesky)/cholesky | solution.py:45
  583.1 0.7 compare_reduce_fusion.3
  583.7 9.8 %custom-call.45 = f32[1,128,128]{1,2,0:T(8,128)S(1)} custom-call(f32[1,128,128]{2,1,0:T(8,128)S(1)} %get-tuple-element.12), custom_call_target="InvertDiagBlocksLowerTriangular" | custom-call | tf_op jit(solution)/shard_map/jit(cholesky)/cholesky | solution.py:45
  593.6 0.9 convolution_dynamic-update-slice_fusion.1
  594.5 1.7 convolution_subtract_fusion.2
  596.2 11.8 %cholesky.375 = f32[128,128]{1,0:T(8,128)S(1)} custom-call(f32[128,128]{1,0:T(8,128)S(1)} %cholesky.444), custom_call_target="Cholesky" | custom-call | tf_op jit(solution)/shard_map/jit(cholesky)/cholesky | solution.py:45
  608.7 0.7 compare_reduce_fusion.2
  609.4 9.8 %custom-call.46 = f32[1,128,128]{1,2,0:T(8,128)S(1)} custom-call(f32[1,128,128]{2,1,0:T(8,128)S(1)} %get-tuple-element.9), custom_call_target="InvertDiagBlocksLowerTriangular" | custom-call | tf_op jit(solution)/shard_map/jit(cholesky)/cholesky | solution.py:45
  619.2 0.9 convolution_dynamic-update-slice_fusion.2
  620.1 1.5 convolution_subtract_fusion.3
  621.6 11.7 %cholesky.394 = f32[128,128]{1,0:T(8,128)S(1)} custom-call(f32[128,128]{1,0:T(8,128)S(1)} %cholesky.449), custom_call_target="Cholesky" | custom-call | tf_op jit(solution)/shard_map/jit(cholesky)/cholesky | solution.py:45
  633.3 0.6 select_reduce_fusion
  633.9 0.7 compare_reduce_fusion.1
  634.6 9.8 %custom-call.47 = f32[1,128,128]{1,2,0:T(8,128)S(1)} custom-call(f32[1,128,128]{2,1,0:T(8,128)S(1)} %get-tuple-element.6), custom_call_target="InvertDiagBlocksLowerTriangular" | custom-call | tf_op jit(solution)/shard_map/jit(cholesky)/cholesky | solution.py:45
  644.4 0.8 convolution_dynamic-update-slice_fusion.3
  645.2 1.2 convolution_subtract_fusion.4
  646.4 2.9 cholesky.415
  649.9 0.7 compare_reduce_fusion
  655.1 1.0 fusion.21
  656.1 0.7 copy.27
  (24 shorter events, 4.0 us)
Async XLA Ops:
  6.5 497.3 %copy-start = (f32[672,672]{1,0:T(8,128)S(1)}, f32[672,672]{1,0:T(8,128)}, u32[]{:S(2)}) copy-start(f32[672,672]{1,0:T(8,128)} %param.5) | copy-start | bytes 5419012
  6.5 497.3 %all-reduce.3.cloned.1.call-start = ((), (), s32[]{:S(2)}) async-start(), calls=%async_computation.2 | async-start | bytes 4128768 | tf_op jit(solution)/shard_map/psum | solution.py:11
  6.5 4.8 copy-start.1
  112.1 12.5 %copy-start.3 = (bf16[672,336]{1,0:T(8,128)(2,1)S(1)}, bf16[672,336]{1,0:T(8,128)(2,1)}, u32[]{:S(2)}) copy-start(bf16[672,336]{1,0:T(8,128)(2,1)} %param.4) | copy-start | bytes 1354756
  517.7 1.3 copy-start.2
Sparse Core Ops, SparseCore 0:
  246.6 257.1 all-reduce.2
